TPU v7x, 256 devices: a whole 4x4x8 slice. The times are simulated.
256 devices in a mesh: node: 64 (over z, x, core), feat: 4 (over y).
Axes of the slice: x: 4, y: 4, z: 8, core: 2. Of those that a mesh axis runs over, the one named last changes fastest.
Arguments:
- features: float32 [49152, 1024], P('node', 'feat'), may hold values from -6 to 6
- degrees: int32 [49152], P('node'), may hold values from 1 to 4
- tile_row: int32 [64, 201], P('node'), may hold values from 0 to 5, as said below
- tile_col: int32 [64, 201], P('node'), may hold values from 0 to 69, as said below
- tile_count: int32 [64], P('node'), may hold values from 75 to 201, as said below
- send_block: int32 [64, 64], replicated, may hold values from 0 to 5
- tile_val: bfloat16 [64, 201, 128, 128], P('node'), may hold values from -0.15625 to 0.15625
- weight: bfloat16 [1024, 3, 1024], P('node', None, 'feat'), may hold values from -0.109375 to 0.109375
- out_bias: float32 [1024], replicated, may hold values from -3 to 3
- cotangent: bfloat16 [49152, 1024], P(('node', 'feat')), may hold values from -0.109375 to 0.109375
Outputs:
- output: bfloat16 [49152, 1024], P(('node', 'feat'))
- weight_grad: float32 [1024, 3, 1024], P('node', None, 'feat')
- bias_grad: float32 [1024], replicated
Inputs may be any that keep to these rules, and one draw needn't show every extreme that they name: `tile_row`: the row block of each slot; for each other part q, between 1 and 3 live tiles of part p read slot 6 + q, each at a different row block. `tile_col`: below 6: the part's own row block; 6 + q: the block that part q sends; the first 12 slots of each part read own blocks, tile i < 6 at row block i, column i; slots past tile_count read 0; no tile reads slot 6 + p in part p. `tile_count`: live tiles come first in each part; some part has 201 live tiles.
All inputs are finite; a program needn't handle non-finite values.
Results may differ from a plain program's by a relative error of at most 0.0057.
Values may be sent and summed in bfloat16 or wider, within the bound.
No kernel may reach another device: no remote copies, remote signals or barrier semaphores. Data moves between devices by JAX's collectives and lax.ppermute only.
A program may use at most 192 MiB of HBM per device.

v0:
```python
import jax
import jax.numpy as jnp
from jax import lax
from jax.sharding import Mesh
from jax.sharding import PartitionSpec as P

HOPS = 2
NODE = ("node_0", "node_1", "node_2")
NODE_FEAT = ("node_0", "node_1", "node_2", "feat")


def sent_to_all(shard, axis):
    devices = lax.axis_size(axis)
    return lax.all_to_all(
        jnp.broadcast_to(shard[None], (devices, *shard.shape)), axis, 0, 0, tiled=True
    )


def laid_out(blocks, dim):
    dims = list(blocks.shape[1:])
    dims[dim] *= blocks.shape[0]
    return jnp.moveaxis(blocks, 0, dim).reshape(dims)


def collect(shard, axis, dim):
    blocks = sent_to_all(shard, axis)
    return laid_out(blocks, dim)


def split_up(shard, dim, devices):
    dims = shard.shape
    blocks = shard.reshape(*dims[:dim], devices, dims[dim] // devices, *dims[dim + 1 :])
    return jnp.moveaxis(blocks, dim, 0)


def sum_at_owner(shard, axis, dim):
    devices = lax.axis_size(axis)
    blocks = lax.all_to_all(split_up(shard, dim, devices), axis, 0, 0, tiled=True)
    return jnp.sum(blocks, axis=0)


def over_axes(shard, axes):
    for axis in axes:
        shard = lax.psum(shard, axis)
    return shard


def propagate(source, tile_rows, tile_cols, tile_values, is_live, send_row):
    block_size = tile_values.shape[-1]
    panel_width = source.shape[1]
    own_blocks = source.reshape(-1, block_size, panel_width)
    outgoing = own_blocks[send_row]
    arrived = lax.all_to_all(outgoing, NODE, split_axis=0, concat_axis=0, tiled=True)
    frame = jnp.concatenate([own_blocks, arrived], axis=0)
    sources = frame[tile_cols]
    product = jnp.einsum("tij,tjc->tic", tile_values, sources, preferred_element_type=jnp.float32)
    block_ids = jnp.arange(own_blocks.shape[0], dtype=jnp.int32)
    onehot = ((tile_rows[:, None] == block_ids[None, :]) & is_live[:, None]).astype(jnp.float32)
    summed = jnp.einsum("tr,tic->ric", onehot, product, precision=lax.Precision.HIGHEST)
    return summed.reshape(source.shape[0], panel_width)


def local(
    features,
    degrees,
    tile_row,
    tile_col,
    tile_count,
    send_block,
    tile_val,
    weight,
    out_bias,
    cotangent,
):
    node_index = lax.axis_index(NODE)
    send_row = lax.dynamic_index_in_dim(send_block, node_index, 0, keepdims=False)
    tile_rows = tile_row[0]
    tile_cols = tile_col[0]
    tile_values = tile_val[0]
    is_live = jnp.arange(tile_rows.shape[0], dtype=jnp.int32) < tile_count[0]
    row_scale = lax.rsqrt(degrees.astype(jnp.float32))[:, None]
    source = (features * row_scale).astype(jnp.bfloat16)
    hop_list = [features.astype(jnp.bfloat16)]
    for hop_number in range(HOPS):
        summed = propagate(source, tile_rows, tile_cols, tile_values, is_live, send_row)
        hop_list.append((summed * row_scale).astype(jnp.bfloat16))
        if hop_number + 1 < HOPS:
            source = (summed * row_scale * row_scale).astype(jnp.bfloat16)
    stacked = jnp.stack(hop_list, axis=1)
    hop_total = stacked.shape[1]
    flat_rows = stacked.reshape(stacked.shape[0], -1)
    piece = collect(weight, NODE, 0)
    flat_piece = piece.reshape(piece.shape[0], -1)
    panel_terms = lax.dot_general(
        flat_rows, flat_piece, (((1,), (1,)), ((), ())), preferred_element_type=jnp.float32
    )
    linear = sum_at_owner(panel_terms, "feat", 0)
    linear = linear + out_bias[None, :]
    sigmoid_val = jax.nn.sigmoid(linear)
    output = (linear * sigmoid_val).astype(jnp.bfloat16)
    grad_linear = (
        cotangent.astype(jnp.float32) * sigmoid_val * (1.0 + linear * (1.0 - sigmoid_val))
    ).astype(jnp.bfloat16)
    bias_grad = over_axes(jnp.sum(grad_linear.astype(jnp.float32), axis=0), NODE_FEAT)
    grad_all = collect(grad_linear, "feat", 0)
    term = lax.dot_general(
        grad_all, flat_rows, (((0,), (0,)), ((), ())), preferred_element_type=jnp.float32
    )
    weight_grad = sum_at_owner(
        term.reshape(weight.shape[0] * lax.axis_size(NODE), hop_total, -1), NODE, 0
    )
    return (output, weight_grad, bias_grad)


def solution(mesh):
    split = Mesh(
        mesh.devices.reshape(8, 4, 2, mesh.shape["feat"]), ("node_0", "node_1", "node_2", "feat")
    )
    return jax.shard_map(
        local,
        mesh=split,
        in_specs=(
            P(NODE, "feat"),
            P(NODE),
            P(NODE, None),
            P(NODE, None),
            P(NODE),
            P(),
            P(NODE, None, None, None),
            P(NODE, None, "feat"),
            P(),
            P(NODE_FEAT, None),
        ),
        out_specs=(P(NODE_FEAT, None), P(NODE, None, "feat"), P()),
        check_vma=False,
    )
```

profile of v0, /device:TPU:8, one launch (start us, length us, event | category | flops | bytes accessed | tf_op | source)
XLA Modules:
  0.0 572.4 jit_solution(15767024178187781781)
XLA Ops:
  2.0 2.3 convert_bitcast_fusion
  4.3 2.8 gather_fusion
  7.1 12.3 %all-to-all-start = ((bf16[64,128,256]{2,1,0:T(8,128)(2,1)}), bf16[64,128,256]{2,1,0:T(8,128)(2,1)}, u32[]{:S(2)}, u32[]{:S(2)}) async-start(bf16[64,128,256]{2,1,0:T(8,128)(2,1)} %gather_fusion), calls=%async_computation | async-start | bytes 8388608 | tf_op jit(solution)/shard_map/all_to_all | solution.py:53
  21.4 94.3 %all-to-all-done = bf16[64,128,256]{2,1,0:T(8,128)(2,1)} async-done(((bf16[64,128,256]{2,1,0:T(8,128)(2,1)}), bf16[64,128,256]{2,1,0:T(8,128)(2,1)}, u32[]{:S(2)}, u32[]{:S(2)}) %all-to-all-start) | async-done | bytes 4194336 | tf_op jit(solution)/shard_map/all_to_all | solution.py:53
  117.0 5.2 all-to-all-start.2
  122.2 4.6 pad_maximum_fusion
  126.9 10.9 %gather_fusion.1 = bf16[201,128,256]{2,1,0:T(8,128)(2,1)} fusion(bf16[70,128,256]{2,1,0:T(8,128)(2,1)} %pad_maximum_fusion, s32[1024]{0:T(1024)S(1)} %pad_clamp_fusion), kind=kCustom, calls=%fused_computation.1 | custom fusion | bytes 26346276 | tf_op jit(solution)/shard_map/gather | solution.py:55
  137.8 16.7 %convolution_bitcast_fusion.1 = f32[201,128,256]{1,2,0:T(8,128)} fusion(bf16[201,128,256]{2,1,0:T(8,128)(2,1)} %gather_fusion.1, bf16[1,201,128,128]{3,2,1,0:T(8,128)(2,1)} %param.16), kind=kOutput, calls=%fused_computation.5 | convolution fusion | flops 1686110208 | bytes 46104576 | tf_op jit(solution)/shard_map/tij,tjc->tic/dot_general | solution.py:56
  154.5 27.1 %copy.38 = f32[201,128,256]{2,0,1:T(8,128)} copy(f32[201,128,256]{1,2,0:T(8,128)} %convolution_bitcast_fusion.1) | data formatting | bytes 52690944 | tf_op jit(solution)/shard_map/tij,tjc->tic/dot_general | solution.py:56
  181.5 13.2 %multiply_convert_fusion = (bf16[6,128,256]{2,0,1:T(8,128)(2,1)S(1)}, f32[6,128,256]{2,0,1:T(8,128)S(1)}) fusion(f32[6,128]{0,1:T(8,128)S(1)} %copy-done.6, f32[201,128,256]{2,0,1:T(8,128)} %copy.38, s32[201]{0:T(256)S(1)} %bitcast.66, pred[201]{0:T(512)(128)(4,1)S(1)} %copy-done.10), kind=kOutput, calls=%fused_computation.13 | convolution fusion | flops 474810752 | bytes 27529196 | tf_op jit(solution)/shard_map/tr,tic->ric/dot_general | solution.py:59
  194.9 2.8 gather_fusion.2
  198.8 10.7 %all-to-all-start.1 = ((bf16[64,128,256]{2,1,0:T(8,128)(2,1)}), bf16[64,128,256]{2,1,0:T(8,128)(2,1)}, u32[]{:S(2)}, u32[]{:S(2)}) async-start(bf16[64,128,256]{2,1,0:T(8,128)(2,1)} %gather_fusion.2), calls=%async_computation.1 | async-start | bytes 8388608 | tf_op jit(solution)/shard_map/all_to_all | solution.py:53
  209.6 2.5 copy.47
  212.1 2.9 reshape.196
  215.2 90.5 %all-to-all-done.1 = bf16[64,128,256]{2,1,0:T(8,128)(2,1)} async-done(((bf16[64,128,256]{2,1,0:T(8,128)(2,1)}), bf16[64,128,256]{2,1,0:T(8,128)(2,1)}, u32[]{:S(2)}, u32[]{:S(2)}) %all-to-all-start.1) | async-done | bytes 4194336 | tf_op jit(solution)/shard_map/all_to_all | solution.py:53
  305.7 4.6 pad_maximum_fusion.1
  310.3 10.9 %gather_fusion.3 = bf16[201,128,256]{2,1,0:T(8,128)(2,1)} fusion(bf16[70,128,256]{2,1,0:T(8,128)(2,1)} %pad_maximum_fusion.1, s32[1024]{0:T(1024)S(1)} %pad_clamp_fusion), kind=kCustom, calls=%fused_computation.3 | custom fusion | bytes 26346276 | tf_op jit(solution)/shard_map/gather | solution.py:55
  321.2 16.7 %convolution_bitcast_fusion = f32[201,128,256]{1,2,0:T(8,128)} fusion(bf16[201,128,256]{2,1,0:T(8,128)(2,1)} %gather_fusion.3, bf16[1,201,128,128]{3,2,1,0:T(8,128)(2,1)} %param.16), kind=kOutput, calls=%fused_computation.4 | convolution fusion | flops 1686110208 | bytes 46104576 | tf_op jit(solution)/shard_map/tij,tjc->tic/dot_general | solution.py:56
  337.9 27.0 %copy.44 = f32[201,128,256]{2,0,1:T(8,128)} copy(f32[201,128,256]{1,2,0:T(8,128)} %convolution_bitcast_fusion) | data formatting | bytes 52690944 | tf_op jit(solution)/shard_map/tij,tjc->tic/dot_general | solution.py:56
  364.9 13.2 %fusion.8 = f32[6,128,256]{2,0,1:T(8,128)S(1)} fusion(f32[201,128,256]{2,0,1:T(8,128)} %copy.44, s32[201]{0:T(256)S(1)} %bitcast.67, pred[201]{0:T(512)(128)(4,1)S(1)} %copy-done.11), kind=kOutput, calls=%fused_computation.27 | convolution fusion | flops 474220928 | bytes 27132908 | tf_op jit(solution)/shard_map/tr,tic->ric/dot_general | solution.py:59
  381.3 2.5 dot_general.38
  383.8 2.7 fusion.18
  386.5 39.5 %all_to_all.30 = f32[4,192,1024]{2,1,0:T(8,128)S(1)} all-to-all(f32[4,192,1024]{2,1,0:T(8,128)S(1)} %fusion.18), channel_id=1, replica_groups=mesh['node_0'=8,'node_1'=4,'node_2'=2,'feat'=4] {'feat'}, dimensions={0} | all-to-all | bytes 6291456 | tf_op jit(solution)/shard_map/all_to_all | solution.py:38
  427.2 2.4 convert_reduce_fusion
  430.9 5.0 all-to-all-start.4
  437.5 15.4 %all-to-all-done.4 = bf16[4,192,1024]{2,1,0:T(8,128)(2,1)S(1)} async-done(((bf16[4,192,1024]{2,1,0:T(8,128)(2,1)}), bf16[4,192,1024]{2,1,0:T(8,128)(2,1)S(1)}, u32[]{:S(2)}, u32[]{:S(2)}) %all-to-all-start.4) | async-done | bytes 1572896 | tf_op jit(solution)/shard_map/all_to_all | solution.py:14
  454.5 4.8 fusion.2
  459.3 9.0 %all-to-all-start.5 = ((f32[64,16,3,256]{3,1,2,0:T(8,128)}), f32[64,16,3,256]{3,1,2,0:T(8,128)S(1)}, u32[]{:S(2)}, u32[]{:S(2)}) async-start(f32[64,16,3,256]{3,1,2,0:T(8,128)} %fusion.2), calls=%async_computation.5 | async-start | bytes 6291456 | tf_op jit(solution)/shard_map/all_to_all | solution.py:38
  468.3 80.4 %psum.28 = f32[1024]{0:T(1024)S(1)} all-reduce(f32[1024]{0:T(1024)S(1)} %get-tuple-element.3), channel_id=1, replica_groups=mesh['node_0'=8,'node_1'=4,'node_2'=2,'feat'=4] {'node_0'}, use_global_device_ids=true, to_apply=%region_3.4 | all-reduce | flops 1024 | bytes 8192 | tf_op jit(solution)/shard_map/psum | solution.py:44
  548.7 10.7 %psum.29 = f32[1024]{0:T(1024)S(1)} all-reduce(f32[1024]{0:T(1024)S(1)} %psum.28), channel_id=1, replica_groups=mesh['node_0'=8,'node_1'=4,'node_2'=2,'feat'=4] {'node_1'}, use_global_device_ids=true, to_apply=%region_4.5 | all-reduce | flops 1024 | bytes 8192 | tf_op jit(solution)/shard_map/psum | solution.py:44
  559.4 2.5 psum.30
  561.9 9.7 %psum.31 = f32[1024]{0:T(1024)} all-reduce(f32[1024]{0:T(1024)S(1)} %psum.30), channel_id=1, replica_groups=mesh['node_0'=8,'node_1'=4,'node_2'=2,'feat'=4] {'feat'}, use_global_device_ids=true, to_apply=%region_6.7 | all-reduce | flops 1024 | bytes 8192 | tf_op jit(solution)/shard_map/psum | solution.py:44
  (47 shorter events, 15.2 us)
Async XLA Ops:
  7.1 14.2 %copy-start.12 = (s32[1,201]{1,0:T(1,128)S(1)}, s32[1,201]{1,0:T(1,128)}, u32[]{:S(2)}) copy-start(s32[1,201]{1,0:T(1,128)} %param.13) | copy-start | bytes 2416
  7.1 108.6 %copy-start.7 = (bf16[16,3,256]{2,0,1:T(8,128)(2,1)S(1)}, bf16[16,3,256]{2,0,1:T(8,128)(2,1)}, u32[]{:S(2)}) copy-start(bf16[16,3,256]{2,0,1:T(8,128)(2,1)} %param.17) | copy-start | bytes 73732
  7.1 108.6 %all-to-all-start = ((bf16[64,128,256]{2,1,0:T(8,128)(2,1)}), bf16[64,128,256]{2,1,0:T(8,128)(2,1)}, u32[]{:S(2)}, u32[]{:S(2)}) async-start(bf16[64,128,256]{2,1,0:T(8,128)(2,1)} %gather_fusion), calls=%async_computation | async-start | bytes 8388608 | tf_op jit(solution)/shard_map/all_to_all | solution.py:53
  117.0 80.6 %all-to-all-start.2 = ((bf16[64,16,3,256]{3,1,2,0:T(8,128)(2,1)}), bf16[64,16,3,256]{3,1,2,0:T(8,128)(2,1)S(1)}, u32[]{:S(2)}, u32[]{:S(2)}) async-start(bf16[64,16,3,256]{3,1,2,0:T(8,128)(2,1)} %broadcast_in_dim.4), calls=%async_computation.2 | async-start | bytes 3145728 | tf_op jit(solution)/shard_map/all_to_all | solution.py:14
  154.5 27.1 %copy-start.6 = (f32[6,128]{0,1:T(8,128)S(1)}, f32[6,128]{0,1:T(8,128)}, u32[]{:S(2)}) copy-start(f32[6,128]{0,1:T(8,128)} %copy.40) | copy-start | bytes 9220
  154.5 27.1 %copy-start.8 = (s32[1,201]{1,0:T(1,128)S(1)}, s32[1,201]{1,0:T(1,128)}, u32[]{:S(2)}) copy-start(s32[1,201]{1,0:T(1,128)} %param.12) | copy-start | bytes 2416
  154.5 27.1 %copy-start.10 = (pred[201]{0:T(512)(128)(4,1)S(1)}, pred[201]{0:T(512)(128)(4,1)}, u32[]{:S(2)}) copy-start(pred[201]{0:T(512)(128)(4,1)} %iota_compare_fusion.1) | copy-start | bytes 607
  197.6 1.2 copy-start.2
  198.8 106.9 %all-to-all-start.1 = ((bf16[64,128,256]{2,1,0:T(8,128)(2,1)}), bf16[64,128,256]{2,1,0:T(8,128)(2,1)}, u32[]{:S(2)}, u32[]{:S(2)}) async-start(bf16[64,128,256]{2,1,0:T(8,128)(2,1)} %gather_fusion.2), calls=%async_computation.1 | async-start | bytes 8388608 | tf_op jit(solution)/shard_map/all_to_all | solution.py:53
  337.9 27.0 %copy-start.11 = (pred[201]{0:T(512)(128)(4,1)S(1)}, pred[201]{0:T(512)(128)(4,1)}, u32[]{:S(2)}) copy-start(pred[201]{0:T(512)(128)(4,1)} %iota_compare_fusion.1) | copy-start | bytes 607
  378.1 1.0 copy-start.4
  378.6 5.2 copy-start.3
  379.3 1.0 copy-start
  386.5 40.7 %copy-start.5 = (bf16[192,1024]{1,0:T(8,128)(2,1)S(1)}, bf16[192,1024]{1,0:T(8,128)(2,1)}, u32[]{:S(2)}) copy-start(bf16[192,1024]{1,0:T(8,128)(2,1)} %param.19) | copy-start | bytes 1179652
  386.5 40.7 %copy-start.9 = (f32[1024]{0:T(1024)S(1)}, f32[1024]{0:T(1024)}, u32[]{:S(2)}) copy-start(f32[1024]{0:T(1024)} %param.18) | copy-start | bytes 12292
  427.2 8.7 %copy-start.1 = (bf16[768,3,256]{2,0,1:T(8,128)(2,1)S(1)}, bf16[768,3,256]{2,0,1:T(8,128)(2,1)}, u32[]{:S(2)}) copy-start(bf16[768,3,256]{2,0,1:T(8,128)(2,1)} %copy-done) | copy-start | bytes 3538948
  430.9 22.0 %all-to-all-start.4 = ((bf16[4,192,1024]{2,1,0:T(8,128)(2,1)}), bf16[4,192,1024]{2,1,0:T(8,128)(2,1)S(1)}, u32[]{:S(2)}, u32[]{:S(2)}) async-start(bf16[4,192,1024]{2,1,0:T(8,128)(2,1)} %broadcast_in_dim.5), calls=%async_computation.4 | async-start | bytes 3145728 | tf_op jit(solution)/shard_map/all_to_all | solution.py:14
  459.3 112.3 %all-to-all-start.5 = ((f32[64,16,3,256]{3,1,2,0:T(8,128)}), f32[64,16,3,256]{3,1,2,0:T(8,128)S(1)}, u32[]{:S(2)}, u32[]{:S(2)}) async-start(f32[64,16,3,256]{3,1,2,0:T(8,128)} %fusion.2), calls=%async_computation.5 | async-start | bytes 6291456 | tf_op jit(solution)/shard_map/all_to_all | solution.py:38
where the time goes:
time: 574 us; the launch traced here: 572 us
  waiting for transfers between devices  200 us (35%)
  blocking collectives  143 us (25%)
  local copies, waits for them, and re-layouts  100 us (17%)
  matrix products  67.3 us (12%)
  starting transfers between devices  42.3 us (7%)
  other arithmetic  18.2 us (3%)
    all_to_all x2, waiting for transfers between devices, propagate(): lax.all_to_all(outgoing, NODE, split_axis=0, concat_axis=0, tiled=True)  185 us
    psum x4, blocking collectives, over_axes(): shard = lax.psum(shard, axis)  103 us
    dot_general x2, local copies, waits for them, and re-layouts, propagate(): jnp.einsum('tij,tjc->tic', tile_values, sources, preferred_element_type=j...  54.1 us
    all_to_all x1, blocking collectives, sum_at_owner(): lax.all_to_all(split_up(shard, dim, devices), axis, 0, 0, tiled=True)  39.5 us
    dot_general x2, matrix products, propagate(): jnp.einsum('tij,tjc->tic', tile_values, sources, preferred_element_type=j...  33.4 us
    dot_general x2, matrix products, propagate(): jnp.einsum('tr,tic->ric', onehot, product, precision=lax.Precision.HIGHEST)  26.4 us
    all_to_all x2, starting transfers between devices, propagate(): lax.all_to_all(outgoing, NODE, split_axis=0, concat_axis=0, tiled=True)  23.1 us
    gather x2, local copies, waits for them, and re-layouts, propagate(): sources = frame[tile_cols]  21.8 us
  transfers between devices with their start and end apart: 5, of which 3 were waited for; matrix products, arithmetic and copies ran while one was open for 15% of the time, Pallas kernels for 0%

commit v1 on v0

--- a/solution.py
+++ b/solution.py
@@ -41,7 +41,7 @@
 
 def over_axes(shard, axes):
     for axis in axes:
-        shard = lax.psum(shard, axis)
+        shard = jnp.sum(lax.all_gather(shard, axis), axis=0)
     return shard
 
 

time: 574 us -> 587 us (1.023)
  blocking collectives: 143 us -> 154 us
    all_gather x0 -> x4, blocking collectives: none -> 114 us  [over_axes(): shard = jnp.sum(lax.all_gather(shard, axis), axis=0)]
    psum x4 -> x0, blocking collectives: 103 us -> none  [over_axes(): shard = lax.psum(shard, axis)]
  transfers between devices with their start and end apart: 5 -> 5, of which waited for: 3 -> 3; matrix products, arithmetic and copies ran while one was open for 15% -> 14% of each run, Pallas kernels for 0% -> 0%
where the time goes in v1:
time: 587 us; the launch traced here: 584 us
  waiting for transfers between devices  200 us (34%)
  blocking collectives  154 us (26%)
  local copies, waits for them, and re-layouts  100 us (17%)
  matrix products  67.3 us (11%)
  starting transfers between devices  42.3 us (7%)
  other arithmetic  18.9 us (3%)
    all_to_all x2, waiting for transfers between devices, propagate(): lax.all_to_all(outgoing, NODE, split_axis=0, concat_axis=0, tiled=True)  185 us
    all_gather x4, blocking collectives, over_axes(): shard = jnp.sum(lax.all_gather(shard, axis), axis=0)  114 us
    dot_general x2, local copies, waits for them, and re-layouts, propagate(): jnp.einsum('tij,tjc->tic', tile_values, sources, preferred_element_type=j...  54.1 us
    all_to_all x1, blocking collectives, sum_at_owner(): lax.all_to_all(split_up(shard, dim, devices), axis, 0, 0, tiled=True)  39.5 us
    dot_general x2, matrix products, propagate(): jnp.einsum('tij,tjc->tic', tile_values, sources, preferred_element_type=j...  33.4 us
    dot_general x2, matrix products, propagate(): jnp.einsum('tr,tic->ric', onehot, product, precision=lax.Precision.HIGHEST)  26.4 us
    all_to_all x2, starting transfers between devices, propagate(): lax.all_to_all(outgoing, NODE, split_axis=0, concat_axis=0, tiled=True)  23.1 us
    gather x2, local copies, waits for them, and re-layouts, propagate(): sources = frame[tile_cols]  21.8 us
  transfers between devices with their start and end apart: 5, of which 3 were waited for; matrix products, arithmetic and copies ran while one was open for 14% of the time, Pallas kernels for 0%

profile of v1, /device:TPU:8, one launch (start us, length us, event | category | flops | bytes accessed | tf_op | source)
XLA Modules:
  0.0 584.3 jit_solution(17139122735311222749)
XLA Ops:
  2.0 2.3 convert_bitcast_fusion
  4.3 2.8 gather_fusion
  7.1 12.3 %all-to-all-start = ((bf16[64,128,256]{2,1,0:T(8,128)(2,1)}), bf16[64,128,256]{2,1,0:T(8,128)(2,1)}, u32[]{:S(2)}, u32[]{:S(2)}) async-start(bf16[64,128,256]{2,1,0:T(8,128)(2,1)} %gather_fusion), calls=%async_computation | async-start | bytes 8388608 | tf_op jit(solution)/shard_map/all_to_all | solution.py:53
  21.4 94.3 %all-to-all-done = bf16[64,128,256]{2,1,0:T(8,128)(2,1)} async-done(((bf16[64,128,256]{2,1,0:T(8,128)(2,1)}), bf16[64,128,256]{2,1,0:T(8,128)(2,1)}, u32[]{:S(2)}, u32[]{:S(2)}) %all-to-all-start) | async-done | bytes 4194336 | tf_op jit(solution)/shard_map/all_to_all | solution.py:53
  117.0 5.2 all-to-all-start.2
  122.2 4.6 pad_maximum_fusion
  126.9 10.9 %gather_fusion.1 = bf16[201,128,256]{2,1,0:T(8,128)(2,1)} fusion(bf16[70,128,256]{2,1,0:T(8,128)(2,1)} %pad_maximum_fusion, s32[1024]{0:T(1024)S(1)} %pad_clamp_fusion), kind=kCustom, calls=%fused_computation.1 | custom fusion | bytes 26346276 | tf_op jit(solution)/shard_map/gather | solution.py:55
  137.8 16.7 %convolution_bitcast_fusion.1 = f32[201,128,256]{1,2,0:T(8,128)} fusion(bf16[201,128,256]{2,1,0:T(8,128)(2,1)} %gather_fusion.1, bf16[1,201,128,128]{3,2,1,0:T(8,128)(2,1)} %param.16), kind=kOutput, calls=%fused_computation.5 | convolution fusion | flops 1686110208 | bytes 46104576 | tf_op jit(solution)/shard_map/tij,tjc->tic/dot_general | solution.py:56
  154.5 27.1 %copy.51 = f32[201,128,256]{2,0,1:T(8,128)} copy(f32[201,128,256]{1,2,0:T(8,128)} %convolution_bitcast_fusion.1) | data formatting | bytes 52690944 | tf_op jit(solution)/shard_map/tij,tjc->tic/dot_general | solution.py:56
  181.5 13.2 %multiply_convert_fusion = (bf16[6,128,256]{2,0,1:T(8,128)(2,1)S(1)}, f32[6,128,256]{2,0,1:T(8,128)S(1)}) fusion(f32[6,128]{0,1:T(8,128)S(1)} %copy-done.6, f32[201,128,256]{2,0,1:T(8,128)} %copy.51, s32[201]{0:T(256)S(1)} %bitcast.66, pred[201]{0:T(512)(128)(4,1)S(1)} %copy-done.10), kind=kOutput, calls=%fused_computation.13 | convolution fusion | flops 474810752 | bytes 27529196 | tf_op jit(solution)/shard_map/tr,tic->ric/dot_general | solution.py:59
  194.9 2.8 gather_fusion.2
  198.8 10.7 %all-to-all-start.1 = ((bf16[64,128,256]{2,1,0:T(8,128)(2,1)}), bf16[64,128,256]{2,1,0:T(8,128)(2,1)}, u32[]{:S(2)}, u32[]{:S(2)}) async-start(bf16[64,128,256]{2,1,0:T(8,128)(2,1)} %gather_fusion.2), calls=%async_computation.1 | async-start | bytes 8388608 | tf_op jit(solution)/shard_map/all_to_all | solution.py:53
  209.6 2.5 copy.60
  212.1 2.9 reshape.200
  215.2 90.5 %all-to-all-done.1 = bf16[64,128,256]{2,1,0:T(8,128)(2,1)} async-done(((bf16[64,128,256]{2,1,0:T(8,128)(2,1)}), bf16[64,128,256]{2,1,0:T(8,128)(2,1)}, u32[]{:S(2)}, u32[]{:S(2)}) %all-to-all-start.1) | async-done | bytes 4194336 | tf_op jit(solution)/shard_map/all_to_all | solution.py:53
  305.7 4.6 pad_maximum_fusion.1
  310.3 10.9 %gather_fusion.3 = bf16[201,128,256]{2,1,0:T(8,128)(2,1)} fusion(bf16[70,128,256]{2,1,0:T(8,128)(2,1)} %pad_maximum_fusion.1, s32[1024]{0:T(1024)S(1)} %pad_clamp_fusion), kind=kCustom, calls=%fused_computation.3 | custom fusion | bytes 26346276 | tf_op jit(solution)/shard_map/gather | solution.py:55
  321.2 16.7 %convolution_bitcast_fusion = f32[201,128,256]{1,2,0:T(8,128)} fusion(bf16[201,128,256]{2,1,0:T(8,128)(2,1)} %gather_fusion.3, bf16[1,201,128,128]{3,2,1,0:T(8,128)(2,1)} %param.16), kind=kOutput, calls=%fused_computation.4 | convolution fusion | flops 1686110208 | bytes 46104576 | tf_op jit(solution)/shard_map/tij,tjc->tic/dot_general | solution.py:56
  337.9 27.0 %copy.57 = f32[201,128,256]{2,0,1:T(8,128)} copy(f32[201,128,256]{1,2,0:T(8,128)} %convolution_bitcast_fusion) | data formatting | bytes 52690944 | tf_op jit(solution)/shard_map/tij,tjc->tic/dot_general | solution.py:56
  364.9 13.2 %fusion.8 = f32[6,128,256]{2,0,1:T(8,128)S(1)} fusion(f32[201,128,256]{2,0,1:T(8,128)} %copy.57, s32[201]{0:T(256)S(1)} %bitcast.67, pred[201]{0:T(512)(128)(4,1)S(1)} %copy-done.11), kind=kOutput, calls=%fused_computation.27 | convolution fusion | flops 474220928 | bytes 27132908 | tf_op jit(solution)/shard_map/tr,tic->ric/dot_general | solution.py:59
  381.3 2.5 dot_general.38
  383.8 2.7 fusion.18
  386.5 39.5 %all_to_all.30 = f32[4,192,1024]{2,1,0:T(8,128)S(1)} all-to-all(f32[4,192,1024]{2,1,0:T(8,128)S(1)} %fusion.18), channel_id=1, replica_groups=mesh['node_0'=8,'node_1'=4,'node_2'=2,'feat'=4] {'feat'}, dimensions={0} | all-to-all | bytes 6291456 | tf_op jit(solution)/shard_map/all_to_all | solution.py:38
  427.2 2.4 convert_reduce_fusion
  430.9 5.0 all-to-all-start.4
  437.5 15.4 %all-to-all-done.4 = bf16[4,192,1024]{2,1,0:T(8,128)(2,1)S(1)} async-done(((bf16[4,192,1024]{2,1,0:T(8,128)(2,1)}), bf16[4,192,1024]{2,1,0:T(8,128)(2,1)S(1)}, u32[]{:S(2)}, u32[]{:S(2)}) %all-to-all-start.4) | async-done | bytes 1572896 | tf_op jit(solution)/shard_map/all_to_all | solution.py:14
  454.5 4.8 fusion.2
  459.3 9.0 %all-to-all-start.5 = ((f32[64,16,3,256]{3,1,2,0:T(8,128)}), f32[64,16,3,256]{3,1,2,0:T(8,128)S(1)}, u32[]{:S(2)}, u32[]{:S(2)}) async-start(f32[64,16,3,256]{3,1,2,0:T(8,128)} %fusion.2), calls=%async_computation.5 | async-start | bytes 6291456 | tf_op jit(solution)/shard_map/all_to_all | solution.py:38
  468.3 88.9 %all-gather = f32[8192]{0:T(1024)S(1)} all-gather(f32[1024]{0:T(1024)S(1)} %get-tuple-element.3), channel_id=2, replica_groups=mesh['node_0'=8,'node_1'=4,'node_2'=2,'feat'=4] {'node_0'}, dimensions={0}, use_global_device_ids=true | all-gather | bytes 36864 | tf_op jit(solution)/shard_map/all_gather | solution.py:44
  557.2 12.3 %all-gather.1 = f32[4096]{0:T(1024)S(1)} all-gather(f32[1024]{0:T(1024)S(1)} %reduce_sum.66), channel_id=3, replica_groups=mesh['node_0'=8,'node_1'=4,'node_2'=2,'feat'=4] {'node_1'}, dimensions={0}, use_global_device_ids=true | all-gather | bytes 20480 | tf_op jit(solution)/shard_map/all_gather | solution.py:44
  569.6 1.8 all-gather.2
  571.5 11.4 %all-gather.3 = f32[4096]{0:T(1024)S(1)} all-gather(f32[1024]{0:T(1024)S(1)} %reduce_sum.68), channel_id=5, replica_groups=mesh['node_0'=8,'node_1'=4,'node_2'=2,'feat'=4] {'feat'}, dimensions={0}, use_global_device_ids=true | all-gather | bytes 20480 | tf_op jit(solution)/shard_map/all_gather | solution.py:44
  (55 shorter events, 15.9 us)
Async XLA Ops:
  7.1 14.2 %copy-start.12 = (s32[1,201]{1,0:T(1,128)S(1)}, s32[1,201]{1,0:T(1,128)}, u32[]{:S(2)}) copy-start(s32[1,201]{1,0:T(1,128)} %param.13) | copy-start | bytes 2416
  7.1 108.6 %copy-start.7 = (bf16[16,3,256]{2,0,1:T(8,128)(2,1)S(1)}, bf16[16,3,256]{2,0,1:T(8,128)(2,1)}, u32[]{:S(2)}) copy-start(bf16[16,3,256]{2,0,1:T(8,128)(2,1)} %param.17) | copy-start | bytes 73732
  7.1 108.6 %all-to-all-start = ((bf16[64,128,256]{2,1,0:T(8,128)(2,1)}), bf16[64,128,256]{2,1,0:T(8,128)(2,1)}, u32[]{:S(2)}, u32[]{:S(2)}) async-start(bf16[64,128,256]{2,1,0:T(8,128)(2,1)} %gather_fusion), calls=%async_computation | async-start | bytes 8388608 | tf_op jit(solution)/shard_map/all_to_all | solution.py:53
  117.0 80.6 %all-to-all-start.2 = ((bf16[64,16,3,256]{3,1,2,0:T(8,128)(2,1)}), bf16[64,16,3,256]{3,1,2,0:T(8,128)(2,1)S(1)}, u32[]{:S(2)}, u32[]{:S(2)}) async-start(bf16[64,16,3,256]{3,1,2,0:T(8,128)(2,1)} %broadcast_in_dim.4), calls=%async_computation.2 | async-start | bytes 3145728 | tf_op jit(solution)/shard_map/all_to_all | solution.py:14
  154.5 27.1 %copy-start.6 = (f32[6,128]{0,1:T(8,128)S(1)}, f32[6,128]{0,1:T(8,128)}, u32[]{:S(2)}) copy-start(f32[6,128]{0,1:T(8,128)} %copy.53) | copy-start | bytes 9220
  154.5 27.1 %copy-start.8 = (s32[1,201]{1,0:T(1,128)S(1)}, s32[1,201]{1,0:T(1,128)}, u32[]{:S(2)}) copy-start(s32[1,201]{1,0:T(1,128)} %param.12) | copy-start | bytes 2416
  154.5 27.1 %copy-start.10 = (pred[201]{0:T(512)(128)(4,1)S(1)}, pred[201]{0:T(512)(128)(4,1)}, u32[]{:S(2)}) copy-start(pred[201]{0:T(512)(128)(4,1)} %iota_compare_fusion.1) | copy-start | bytes 607
  197.6 1.2 copy-start.2
  198.8 106.9 %all-to-all-start.1 = ((bf16[64,128,256]{2,1,0:T(8,128)(2,1)}), bf16[64,128,256]{2,1,0:T(8,128)(2,1)}, u32[]{:S(2)}, u32[]{:S(2)}) async-start(bf16[64,128,256]{2,1,0:T(8,128)(2,1)} %gather_fusion.2), calls=%async_computation.1 | async-start | bytes 8388608 | tf_op jit(solution)/shard_map/all_to_all | solution.py:53
  337.9 27.0 %copy-start.11 = (pred[201]{0:T(512)(128)(4,1)S(1)}, pred[201]{0:T(512)(128)(4,1)}, u32[]{:S(2)}) copy-start(pred[201]{0:T(512)(128)(4,1)} %iota_compare_fusion.1) | copy-start | bytes 607
  378.1 1.0 copy-start.4
  378.6 5.2 copy-start.3
  379.3 1.0 copy-start
  386.5 40.7 %copy-start.5 = (bf16[192,1024]{1,0:T(8,128)(2,1)S(1)}, bf16[192,1024]{1,0:T(8,128)(2,1)}, u32[]{:S(2)}) copy-start(bf16[192,1024]{1,0:T(8,128)(2,1)} %param.19) | copy-start | bytes 1179652
  386.5 40.7 %copy-start.9 = (f32[1024]{0:T(1024)S(1)}, f32[1024]{0:T(1024)}, u32[]{:S(2)}) copy-start(f32[1024]{0:T(1024)} %param.18) | copy-start | bytes 12292
  427.2 8.7 %copy-start.1 = (bf16[768,3,256]{2,0,1:T(8,128)(2,1)S(1)}, bf16[768,3,256]{2,0,1:T(8,128)(2,1)}, u32[]{:S(2)}) copy-start(bf16[768,3,256]{2,0,1:T(8,128)(2,1)} %copy-done) | copy-start | bytes 3538948
  430.9 22.0 %all-to-all-start.4 = ((bf16[4,192,1024]{2,1,0:T(8,128)(2,1)}), bf16[4,192,1024]{2,1,0:T(8,128)(2,1)S(1)}, u32[]{:S(2)}, u32[]{:S(2)}) async-start(bf16[4,192,1024]{2,1,0:T(8,128)(2,1)} %broadcast_in_dim.5), calls=%async_computation.4 | async-start | bytes 3145728 | tf_op jit(solution)/shard_map/all_to_all | solution.py:14
  459.3 124.2 %all-to-all-start.5 = ((f32[64,16,3,256]{3,1,2,0:T(8,128)}), f32[64,16,3,256]{3,1,2,0:T(8,128)S(1)}, u32[]{:S(2)}, u32[]{:S(2)}) async-start(f32[64,16,3,256]{3,1,2,0:T(8,128)} %fusion.2), calls=%async_computation.5 | async-start | bytes 6291456 | tf_op jit(solution)/shard_map/all_to_all | solution.py:38
